TPU v7x, 256 devices: a whole 4x4x8 slice. The times are simulated.
256 devices in a mesh: noise: 8 (over x, y_hi), row: 4 (over y_lo, core), col: 8 (over z).
Axes of the slice: x: 4, y: 4 (y_hi: 2, y_lo: 2; y = y_hi * 2 + y_lo), z: 8, core: 2. Of those that a mesh axis runs over, the one named last changes fastest.
Arguments:
- image: bfloat16 [1024, 256, 128], P(('noise', 'row'), 'col'), parts along dimension 0, may hold values from -6 to 6
- noise_level: int32 [8], P('noise'), parts along dimension 0, may hold values from 0 to 7
- cond_table: float32 [8, 256], replicated, may hold values from -6 to 6
- ada_fine: float32 [256, 128], replicated, may hold values from -0.375 to 0.375
- fine_qkv: bfloat16 [128, 384], replicated, may hold values from -0.5 to 0.5
- fine_scale: float32 [2], replicated, may hold values from 4 to 16
- fine_out_w: bfloat16 [128, 128], replicated, may hold values from -0.5 to 0.5
- fine_post: float32 [128], replicated, may hold values from 0.1 to 1.9
- merge_w: bfloat16 [512, 256], replicated, may hold values from -0.25 to 0.25
- coarse_in_w: bfloat16 [256, 1024], replicated, may hold values from -0.375 to 0.375
- ada_coarse: float32 [256, 1024], replicated, may hold values from -0.375 to 0.375
- coarse_qkv: bfloat16 [3, 1024, 1024], P(None, None, 'col'), may hold values from -0.1875 to 0.1875
- coarse_scale: float32 [16], P('col'), may hold values from 4 to 16
- coarse_out_w: bfloat16 [1024, 1024], P('col'), may hold values from -0.1875 to 0.1875
- coarse_post: float32 [1024], replicated, may hold values from 0.1 to 1.9
Outputs:
- fine_out: bfloat16 [1024, 256, 128], P(('noise', 'row'), 'col'), parts along dimension 0
- coarse_out: bfloat16 [64, 16, 1024], P(('noise', 'row'), 'col'), parts along dimension 0
There are 8 independent parts, one for each index of `noise`. A program takes and returns all parts, laid end to end along the dimension named above; an argument that names none is the same for every part. Nothing has to cross between parts.
All inputs are finite; a program needn't handle non-finite values.
Results may differ from a plain program's by a relative error of at most 0.035.
Values may be sent and summed in bfloat16 or wider, within the bound.
No kernel may reach another device: no remote copies, remote signals or barrier semaphores. Data moves between devices by JAX's collectives and lax.ppermute only.
A program may use at most 128 MiB of HBM per device.

v0:
```python
import jax
import jax.numpy as jnp
from jax import lax
from jax.sharding import PartitionSpec as P

HEAD = 64
TILE = 32
POOL = 8


def with_halo(x, sides, width):
    for axis, dim in sides:
        devices, length = (lax.axis_size(axis), x.shape[dim])
        up = [(i, (i + 1) % devices) for i in range(devices - 1)]
        down = [(j, i) for i, j in up]
        last = lax.slice_in_dim(x, length - width, length, axis=dim)
        initial = lax.slice_in_dim(x, 0, width, axis=dim)
        before = lax.ppermute(last, axis, up)
        after = lax.ppermute(initial, axis, down)
        x = jnp.concatenate([before, x, after], axis=dim)
    return x


def rms(value):
    return value * lax.rsqrt(jnp.mean(value * value, axis=-1, keepdims=True) + 1e-06)


def cosine(value, heads):
    shaped = value.reshape(value.shape[:-1] + (heads, HEAD))
    return rms(shaped).reshape(value.shape)


def attend(queries, keys, values, valid, scale, heads):
    results = []
    for head in range(heads):
        low = head * HEAD
        scores = jnp.dot(
            queries[:, low : low + HEAD],
            keys[:, low : low + HEAD].T,
            preferred_element_type=jnp.float32,
        )
        scores = scores * (scale[head] / HEAD)
        if valid is not None:
            scores = jnp.where(valid[None, :], scores, -jnp.inf)
        top = jnp.max(scores, axis=-1, keepdims=True)
        expo = jnp.exp(scores - top)
        if valid is not None:
            expo = jnp.where(valid[None, :], expo, 0.0)
        weights = (expo / jnp.sum(expo, axis=-1, keepdims=True)).astype(jnp.bfloat16)
        results.append(
            jnp.dot(weights, values[:, low : low + HEAD], preferred_element_type=jnp.float32)
        )
    return jnp.concatenate(results, axis=-1).astype(jnp.bfloat16)


def attend_blocks(queries, keys, values, valid, scale, heads):
    count, width = queries.shape
    block = min(512, count)
    grouped = queries.reshape(count // block, block, width)

    def one_block(part_q):
        return attend(part_q, keys, values, valid, scale, heads)

    return lax.map(one_block, grouped).reshape(count, width)


def body(
    image,
    noise_level,
    cond_table,
    ada_fine,
    fine_qkv,
    fine_scale,
    fine_out_w,
    fine_post,
    merge_w,
    coarse_in_w,
    ada_coarse,
    coarse_qkv,
    coarse_scale,
    coarse_out_w,
    coarse_post,
):
    highest = lax.Precision.HIGHEST
    tile = TILE
    rows_loc, cols_loc, width = image.shape
    heads = width // HEAD
    levels = jnp.arange(cond_table.shape[0], dtype=jnp.int32)
    hot = (levels == noise_level[0]).astype(jnp.float32)
    cond = jnp.dot(hot, cond_table, precision=highest)
    fine_gain = 1.0 + jnp.dot(cond, ada_fine, precision=highest)
    coarse_gain = 1.0 + jnp.dot(cond, ada_coarse, precision=highest)
    xfull = image.astype(jnp.float32)
    xn = (rms(xfull) * fine_gain).astype(jnp.bfloat16)
    qproj = jnp.dot(xn.reshape(-1, width), fine_qkv[:, :width], preferred_element_type=jnp.float32)
    queries = cosine(qproj, heads).astype(jnp.bfloat16).reshape(rows_loc, cols_loc, width)
    shape = xn.shape[:2]
    proj = jnp.dot(xn.reshape(-1, width), fine_qkv[:, width:], preferred_element_type=jnp.float32)
    proj = proj.reshape(shape + (2 * width,))
    keys_out = cosine(proj[..., :width], heads).astype(jnp.bfloat16)
    values_out = proj[..., width:].astype(jnp.bfloat16)
    both = jnp.stack([keys_out, values_out], axis=0)
    padded = with_halo(both, (("row", 1), ("col", 2)), tile)
    keys_pad = padded[0]
    values_pad = padded[1]
    grid_rows = rows_loc * lax.axis_size("row")
    grid_cols = cols_loc * lax.axis_size("col")
    row_ids = (
        lax.axis_index("row") * rows_loc - tile + jnp.arange(rows_loc + 2 * tile, dtype=jnp.int32)
    )
    col_ids = (
        lax.axis_index("col") * cols_loc - tile + jnp.arange(cols_loc + 2 * tile, dtype=jnp.int32)
    )
    row_ok = (row_ids >= 0) & (row_ids < grid_rows)
    col_ok = (col_ids >= 0) & (col_ids < grid_cols)
    q_tile = queries.reshape(tile * tile, width)
    k_win = keys_pad.reshape(-1, width)
    v_win = values_pad.reshape(-1, width)
    valid = (row_ok[:, None] & col_ok[None, 0 : 3 * tile]).reshape(-1)
    result = attend_blocks(q_tile, k_win, v_win, valid, fine_scale, heads)
    pieces = [result.reshape(tile, tile, width)]
    attended = jnp.concatenate(pieces, axis=1)
    branch = jnp.dot(attended.reshape(-1, width), fine_out_w, preferred_element_type=jnp.float32)
    branch = branch.reshape(rows_loc, cols_loc, width)
    fine_out = (xfull + rms(branch) * fine_post).astype(jnp.bfloat16)
    merge_width = merge_w.shape[1]
    blocks = (
        fine_out.reshape(rows_loc // 2, 2, cols_loc // 2, 2, width)
        .transpose(0, 2, 1, 3, 4)
        .reshape(-1, 4 * width)
    )
    merged = jnp.dot(blocks, merge_w, preferred_element_type=jnp.float32).astype(jnp.bfloat16)
    pool_rows = rows_loc // (2 * POOL)
    pool_cols = cols_loc // (2 * POOL)
    merged = merged.reshape(pool_rows, POOL, pool_cols, POOL, merge_width).astype(jnp.float32)
    pooled = jnp.mean(merged, axis=(1, 3)).astype(jnp.bfloat16).reshape(-1, merge_width)
    coarse_in = jnp.dot(pooled, coarse_in_w, preferred_element_type=jnp.float32)
    cn = (rms(coarse_in) * coarse_gain).astype(jnp.bfloat16)
    coarse_width = cn.shape[1]
    local_width = coarse_qkv.shape[2]
    local_heads = local_width // HEAD
    proj = jnp.einsum(
        "nd,kde->kne",
        lax.all_gather(cn, ("row", "col"), axis=0, tiled=True),
        coarse_qkv,
        preferred_element_type=jnp.float32,
    )
    q_part = cosine(proj[0], local_heads)
    k_part = cosine(proj[1], local_heads)
    projected = jnp.concatenate([q_part, k_part, proj[2]], axis=-1).astype(jnp.bfloat16)
    own_count = cn.shape[0]
    row_count = own_count * lax.axis_size("col")
    row_start = lax.axis_index("row") * row_count
    q_rows = lax.dynamic_slice_in_dim(projected[:, :local_width], row_start, row_count, 0)
    k_all = projected[:, local_width : 2 * local_width]
    v_all = projected[:, 2 * local_width :]
    coarse_attended = attend(q_rows, k_all, v_all, None, coarse_scale, local_heads)
    coarse_branch = lax.psum_scatter(
        jnp.dot(coarse_attended, coarse_out_w, preferred_element_type=jnp.float32).astype(
            jnp.bfloat16
        ),
        "col",
        scatter_dimension=0,
        tiled=True,
    ).astype(jnp.float32)
    coarse_out = (coarse_in + rms(coarse_branch) * coarse_post).astype(jnp.bfloat16)
    coarse_out = coarse_out.reshape(pool_rows, pool_cols, coarse_width)
    return (fine_out, coarse_out)


def solution(mesh):
    in_specs = (
        P(("noise", "row"), "col", None),
        P("noise"),
        P(),
        P(),
        P(),
        P(),
        P(),
        P(),
        P(),
        P(),
        P(),
        P(None, None, "col"),
        P("col"),
        P("col", None),
        P(),
    )
    out_specs = (P(("noise", "row"), "col", None), P(("noise", "row"), "col", None))
    return jax.shard_map(body, mesh=mesh, in_specs=in_specs, out_specs=out_specs, check_vma=False)
```

profile of v0, /device:TPU:2, one launch (start us, length us, event | category | flops | bytes accessed | tf_op | source)
XLA Modules:
  0.0 353.1 jit_solution(10420121565007312929)
XLA Ops:
  16.0 1.9 reduce_sum.123
  20.3 2.2 mul.197
  25.1 1.8 collective-permute-start
  28.4 3.6 %collective-permute-done.1 = bf16[2,32,32,128]{3,2,1,0:T(8,128)(2,1)S(1)} collective-permute-done((bf16[2,32,32,128]{3,2,1,0:T(8,128)(2,1)S(1)}, bf16[2,32,32,128]{3,2,1,0:T(8,128)(2,1)S(1)}, u32[]{:S(2)}, u32[]{:S(2)}) %collective-permute-start.1) | collective-permute-done | bytes 524320 | tf_op jit(solution)/shard_map/ppermute | solution.py:19
  33.3 5.0 %collective-permute-start.2 = (bf16[2,96,32,128]{3,2,1,0:T(8,128)(2,1)}, bf16[2,96,32,128]{3,2,1,0:T(8,128)(2,1)}, u32[]{:S(2)}, u32[]{:S(2)}) collective-permute-start(bf16[2,96,32,128]{3,2,1,0:T(8,128)(2,1)} %pad_maximum_fusion.2), channel_id=1, source_target_pairs={{0,1},{1,2},{2,3},{3,4},{4,5},{5,6},{6,7},{8,9},{9,10},{10,11},{11... | collective-permute-start | bytes 4718600 | tf_op jit(solution)/shard_map/ppermute | solution.py:18
  44.7 2.3 copy.42
  50.1 15.4 %collective-permute-done.2 = bf16[2,96,32,128]{3,2,1,0:T(8,128)(2,1)} collective-permute-done((bf16[2,96,32,128]{3,2,1,0:T(8,128)(2,1)}, bf16[2,96,32,128]{3,2,1,0:T(8,128)(2,1)}, u32[]{:S(2)}, u32[]{:S(2)}) %collective-permute-start.2) | collective-permute-done | bytes 1572896 | tf_op jit(solution)/shard_map/ppermute | solution.py:18
  65.6 5.8 %collective-permute-done.3 = bf16[2,96,32,128]{3,2,1,0:T(8,128)(2,1)} collective-permute-done((bf16[2,96,32,128]{3,2,1,0:T(8,128)(2,1)}, bf16[2,96,32,128]{3,2,1,0:T(8,128)(2,1)}, u32[]{:S(2)}, u32[]{:S(2)}) %collective-permute-start.3) | collective-permute-done | bytes 1572896 | tf_op jit(solution)/shard_map/ppermute | solution.py:19
  71.4 8.8 %pad_maximum_fusion.1 = bf16[2,96,96,128]{3,2,1,0:T(8,128)(2,1)S(1)} fusion(bf16[2,96,32,128]{3,2,1,0:T(8,128)(2,1)} %collective-permute-done.3, bf16[2,32,32,128]{3,2,1,0:T(8,128)(2,1)S(1)} %collective-permute-done.1, bf16[1,32,32,128]{3,2,1,0:T(8,128)(2,1)S(1)} %fusion.38, bf16[1,32,32,128]{3,2,1,0:T(8,128)(2,1)S(1)} %fusion.37, ...), kind=kLoop, calls=%fused_computation.33 | loop fusion | flops 28311552 | bytes 9437184 | tf_op jit(solution)/shard_map/concatenate | solution.py:20
  80.2 2.2 fusion.72
  82.5 118.6 %while.13 = (s32[]{:T(128)}, bf16[2,512,128]{2,1,0:T(8,128)(2,1)}, bf16[2,512,128]{2,1,0:T(8,128)(2,1)S(1)}, bf16[9216,128]{1,0:T(8,128)(2,1)S(1)}, f32[]{:T(128...) while((s32[]{:T(128)}, bf16[2,512,128]{2,1,0:T(8,128)(2,1)}, ...), condition=%wide.region_8.9_spmd.clone, body=%wide.region_3.8_spmd.clone.sunk | while | flops 2548374528 | bytes 133657432 | solution.py:64
  82.9 7.8 %fusion.104 = (f32[512]{0:T(512)S(1)}, f32[512,9216]{1,0:T(8,128)}) fusion(f32[]{:T(128)} %get-tuple-element.291, pred[9216]{0:T(1024)(128)(4,1)S(1)} %broadcast_in_dim.143, bf16[9216,128]{1,0:T(8,128)(2,1)S(1)} %get-tuple-element.290, bf16[512,128]{1,0:T(8,128)(2,1)S(1)} %dynamic-slice_bitcast_fusion.2), kind=kOutput, calls=%fused_computation.7.clone.1 | convolution fusion | flops 618135040 | bytes 21376004 | tf_op jit(solution)/shard_map/while/body/eval_jaxpr/dot_general | solution.py:37
  90.7 18.1 %fusion.105 = (f32[512]{0:T(512)S(1)}, f32[512]{0:T(512)S(1)}, f32[512,9216]{1,0:T(8,128)}) fusion(f32[512,9216]{1,0:T(8,128)} %get-tuple-element.262, f32[512]{0:T(512)S(1)} %get-tuple-element.263, f32[]{:T(128)} %get-tuple-element.291, pred[9216]{0:T(1024)(128)(4,1)S(1)} %broadcast_in_dim.143, f32[]{:T(128)} %get-tuple-element.293, ...), kind=kOutput, calls=%fused_computation.9.clone.1 | convolution fusion | flops 641727488 | bytes 40254472 | tf_op jit(solution)/shard_map/while/body/eval_jaxpr/dot_general | solution.py:37
  108.9 9.4 %fusion.108 = bf16[1,512,64]{1,2,0:T(8,128)(2,1)S(1)} fusion(bf16[9216,128]{1,0:T(8,128)(2,1)S(1)} %copy-done.4, f32[512,9216]{1,0:T(8,128)} %get-tuple-element.262, f32[512]{0:T(512)S(1)} %get-tuple-element.266, f32[512]{0:T(512)S(1)} %get-tuple-element.263, f32[]{:T(128)} %get-tuple-element.291, pred[9216]{0:T(1024)(128)(4,1)S(1)} %broadcast_in_dim.143), kind=kOutput, calls=%fused_computation.21.clone.1 | convolution fusion | flops 632324096 | bytes 21312516 | tf_op jit(solution)/shard_map/while/body/eval_jaxpr/dot_general | solution.py:51
  118.3 11.7 %fusion.106 = f32[512]{0:T(512)S(1)} fusion(f32[512,9216]{1,0:T(8,128)} %get-tuple-element.264, f32[512]{0:T(512)S(1)} %get-tuple-element.265, f32[]{:T(128)} %get-tuple-element.293, pred[9216]{0:T(1024)(128)(4,1)S(1)} %broadcast_in_dim.143), kind=kLoop, calls=%fused_computation.10.clone.1 | loop fusion | flops 23592448 | bytes 18887684 | tf_op jit(solution)/shard_map/while/body/eval_jaxpr/reduce_sum | solution.py:49
  130.0 11.1 %fusion.107 = bf16[1,512,64]{1,2,0:T(8,128)(2,1)S(1)} fusion(bf16[9216,128]{1,0:T(8,128)(2,1)} %get-tuple-element.292, f32[512,9216]{1,0:T(8,128)} %get-tuple-element.264, f32[512]{0:T(512)S(1)} %fusion.106, f32[512]{0:T(512)S(1)} %get-tuple-element.265, f32[]{:T(128)} %get-tuple-element.293, pred[9216]{0:T(1024)(128)(4,1)S(1)} %broadcast_in_dim.143), kind=kOutput, calls=%fused_computation.22.clone.1 | convolution fusion | flops 632324096 | bytes 21312516 | tf_op jit(solution)/shard_map/while/body/eval_jaxpr/dot_general | solution.py:51
  142.1 7.8 %fusion.104 = (f32[512]{0:T(512)S(1)}, f32[512,9216]{1,0:T(8,128)}) fusion(f32[]{:T(128)} %get-tuple-element.291, pred[9216]{0:T(1024)(128)(4,1)S(1)} %broadcast_in_dim.143, bf16[9216,128]{1,0:T(8,128)(2,1)S(1)} %get-tuple-element.290, bf16[512,128]{1,0:T(8,128)(2,1)S(1)} %dynamic-slice_bitcast_fusion.2), kind=kOutput, calls=%fused_computation.7.clone.1 | convolution fusion | flops 618135040 | bytes 21376004 | tf_op jit(solution)/shard_map/while/body/eval_jaxpr/dot_general | solution.py:37
  149.9 18.1 %fusion.105 = (f32[512]{0:T(512)S(1)}, f32[512]{0:T(512)S(1)}, f32[512,9216]{1,0:T(8,128)}) fusion(f32[512,9216]{1,0:T(8,128)} %get-tuple-element.262, f32[512]{0:T(512)S(1)} %get-tuple-element.263, f32[]{:T(128)} %get-tuple-element.291, pred[9216]{0:T(1024)(128)(4,1)S(1)} %broadcast_in_dim.143, f32[]{:T(128)} %get-tuple-element.293, ...), kind=kOutput, calls=%fused_computation.9.clone.1 | convolution fusion | flops 641727488 | bytes 40254472 | tf_op jit(solution)/shard_map/while/body/eval_jaxpr/dot_general | solution.py:37
  168.1 9.4 %fusion.108 = bf16[1,512,64]{1,2,0:T(8,128)(2,1)S(1)} fusion(bf16[9216,128]{1,0:T(8,128)(2,1)S(1)} %copy-done.4, f32[512,9216]{1,0:T(8,128)} %get-tuple-element.262, f32[512]{0:T(512)S(1)} %get-tuple-element.266, f32[512]{0:T(512)S(1)} %get-tuple-element.263, f32[]{:T(128)} %get-tuple-element.291, pred[9216]{0:T(1024)(128)(4,1)S(1)} %broadcast_in_dim.143), kind=kOutput, calls=%fused_computation.21.clone.1 | convolution fusion | flops 632324096 | bytes 21312516 | tf_op jit(solution)/shard_map/while/body/eval_jaxpr/dot_general | solution.py:51
  177.5 11.7 %fusion.106 = f32[512]{0:T(512)S(1)} fusion(f32[512,9216]{1,0:T(8,128)} %get-tuple-element.264, f32[512]{0:T(512)S(1)} %get-tuple-element.265, f32[]{:T(128)} %get-tuple-element.293, pred[9216]{0:T(1024)(128)(4,1)S(1)} %broadcast_in_dim.143), kind=kLoop, calls=%fused_computation.10.clone.1 | loop fusion | flops 23592448 | bytes 18887684 | tf_op jit(solution)/shard_map/while/body/eval_jaxpr/reduce_sum | solution.py:49
  189.2 11.1 %fusion.107 = bf16[1,512,64]{1,2,0:T(8,128)(2,1)S(1)} fusion(bf16[9216,128]{1,0:T(8,128)(2,1)} %get-tuple-element.292, f32[512,9216]{1,0:T(8,128)} %get-tuple-element.264, f32[512]{0:T(512)S(1)} %fusion.106, f32[512]{0:T(512)S(1)} %get-tuple-element.265, f32[]{:T(128)} %get-tuple-element.293, pred[9216]{0:T(1024)(128)(4,1)S(1)} %broadcast_in_dim.143), kind=kOutput, calls=%fused_computation.22.clone.1 | convolution fusion | flops 632324096 | bytes 21312516 | tf_op jit(solution)/shard_map/while/body/eval_jaxpr/dot_general | solution.py:51
  206.7 57.0 %all-gather = bf16[32,4,1024]{2,1,0:T(4,128)(2,1)S(1)} all-gather(bf16[1,4,1024]{2,1,0:T(4,128)(2,1)S(1)} %fusion.59), channel_id=1, replica_groups=mesh['noise'=8,'row'=4,'col'=8] {'row','col'}, dimensions={0}, use_global_device_ids=true | all-gather | bytes 270336 | tf_op jit(solution)/shard_map/all_gather | solution.py:144
  266.9 1.8 convolution_convert_fusion.1
  270.0 74.0 %all-reduce.3.cloned.1.call-done = bf16[32,1024]{1,0:T(8,128)(2,1)} async-done(((bf16[32,1024]{1,0:T(8,128)(2,1)}), bf16[32,1024]{1,0:T(8,128)(2,1)}) %all-reduce.3.cloned.1.call-update) | async-done | bytes 65552
  (108 shorter events, 36.2 us)
Async XLA Ops:
  7.2 41.8 %copy-start = (f32[256,1024]{1,0:T(8,128)S(1)}, f32[256,1024]{1,0:T(8,128)}, u32[]{:S(2)}) copy-start(f32[256,1024]{1,0:T(8,128)} %param.27) | copy-start | bytes 3145732
  7.2 336.8 %all-reduce.3.cloned.1.call-start = ((), (), s32[]{:S(2)}) async-start(), calls=%async_computation | async-start | bytes 131072
  12.2 2.1 copy-start.3
  12.2 30.6 %copy-start.9 = (f32[2]{0:T(128)S(1)}, f32[2]{0:T(128)}, u32[]{:S(2)}) copy-start(f32[2]{0:T(128)} %param.22) | copy-start | bytes 28
  13.4 33.6 %copy-start.10 = (f32[2]{0:T(128)S(1)}, f32[2]{0:T(128)}, u32[]{:S(2)}) copy-start(f32[2]{0:T(128)} %param.29) | copy-start | bytes 28
  25.1 3.3 collective-permute-start
  26.9 5.1 %collective-permute-start.1 = (bf16[2,32,32,128]{3,2,1,0:T(8,128)(2,1)S(1)}, bf16[2,32,32,128]{3,2,1,0:T(8,128)(2,1)S(1)}, u32[]{:S(2)}, u32[]{:S(2)}) collective-permute-start(bf16[2,32,32,128]{3,2,1,0:T(8,128)(2,1)S(1)} %pad_maximum_fusion.3), channel_id=1, source_target_pairs={{8,0},{16,8},{24,16},{9,1},{17,9},{25,17},{10,2},{18,10},{26,18},{... | collective-permute-start | bytes 1572872 | tf_op jit(solution)/shard_map/ppermute | solution.py:19
  33.3 32.2 %collective-permute-start.2 = (bf16[2,96,32,128]{3,2,1,0:T(8,128)(2,1)}, bf16[2,96,32,128]{3,2,1,0:T(8,128)(2,1)}, u32[]{:S(2)}, u32[]{:S(2)}) collective-permute-start(bf16[2,96,32,128]{3,2,1,0:T(8,128)(2,1)} %pad_maximum_fusion.2), channel_id=1, source_target_pairs={{0,1},{1,2},{2,3},{3,4},{4,5},{5,6},{6,7},{8,9},{9,10},{10,11},{11... | collective-permute-start | bytes 4718600 | tf_op jit(solution)/shard_map/ppermute | solution.py:18
  38.3 33.1 %collective-permute-start.3 = (bf16[2,96,32,128]{3,2,1,0:T(8,128)(2,1)}, bf16[2,96,32,128]{3,2,1,0:T(8,128)(2,1)}, u32[]{:S(2)}, u32[]{:S(2)}) collective-permute-start(bf16[2,96,32,128]{3,2,1,0:T(8,128)(2,1)} %pad_maximum_fusion.2), channel_id=1, source_target_pairs={{1,0},{2,1},{3,2},{4,3},{5,4},{6,5},{7,6},{9,8},{10,9},{11,10},{12... | collective-permute-start | bytes 4718600 | tf_op jit(solution)/shard_map/ppermute | solution.py:19
  50.1 32.3 %copy-start.2 = (bf16[2,512,128]{2,1,0:T(8,128)(2,1)S(1)}, bf16[2,512,128]{2,1,0:T(8,128)(2,1)}, u32[]{:S(2)}) copy-start(bf16[2,512,128]{2,1,0:T(8,128)(2,1)} %copy.39) | copy-start | bytes 786436
  82.4 118.7 %copy-start.6 = (bf16[128,128]{1,0:T(8,128)(2,1)S(1)}, bf16[128,128]{1,0:T(8,128)(2,1)}, u32[]{:S(2)}) copy-start(bf16[128,128]{1,0:T(8,128)(2,1)} %param.23) | copy-start | bytes 98308
  82.4 120.1 %copy-start.11 = (f32[128]{0:T(128)S(1)}, f32[128]{0:T(128)}, u32[]{:S(2)}) copy-start(f32[128]{0:T(128)} %param.24) | copy-start | bytes 1540
  82.4 124.2 %copy-start.7 = (f32[1024]{0:T(1024)S(1)}, f32[1024]{0:T(1024)}, u32[]{:S(2)}) copy-start(f32[1024]{0:T(1024)} %broadcast_add_fusion) | copy-start | bytes 12292
  82.4 186.3 %copy-start.12 = (u32[256]{0:T(256)S(1)}, u32[256]{0:T(256)}, u32[]{:S(2)}) copy-start(u32[256]{0:T(256)} %constant.97) | copy-start | bytes 3076
  82.5 262.4 %copy-start.8 = (f32[1024]{0:T(1024)S(1)}, f32[1024]{0:T(1024)}, u32[]{:S(2)}) copy-start(f32[1024]{0:T(1024)} %param.31) | copy-start | bytes 12292
  90.7 18.1 %copy-start.4 = (bf16[9216,128]{1,0:T(8,128)(2,1)S(1)}, bf16[9216,128]{1,0:T(8,128)(2,1)}, u32[]{:S(2)}) copy-start(bf16[9216,128]{1,0:T(8,128)(2,1)} %get-tuple-element.292) | copy-start | bytes 7077892 | tf_op jit(solution)/shard_map/while
  149.9 18.1 %copy-start.4 = (bf16[9216,128]{1,0:T(8,128)(2,1)S(1)}, bf16[9216,128]{1,0:T(8,128)(2,1)}, u32[]{:S(2)}) copy-start(bf16[9216,128]{1,0:T(8,128)(2,1)} %get-tuple-element.292) | copy-start | bytes 7077892 | tf_op jit(solution)/shard_map/while
  201.1 145.2 %copy-start.1 = (f32[256,1024]{1,0:T(8,128)S(1)}, f32[256,1024]{1,0:T(8,128)}, u32[]{:S(2)}) copy-start(f32[256,1024]{1,0:T(8,128)} %param.27) | copy-start | bytes 3145732
  203.7 142.6 %copy-start.5 = (bf16[32,32,128]{2,1,0:T(8,128)(2,1)}, bf16[32,32,128]{2,1,0:T(8,128)(2,1)S(1)}, u32[]{:S(2)}) copy-start(bf16[32,32,128]{2,1,0:T(8,128)(2,1)S(1)} %fusion.36) | copy-start | bytes 786436
Sparse Core Ops, SparseCore 0:
  268.9 75.0 all-reduce.2
where the time goes:
time: 354 us; the launch traced here: 353 us
  matrix products  106 us (30%)
  waiting for transfers between devices  99.1 us (28%)
  blocking collectives  57 us (16%)
  other arithmetic  44.3 us (13%)
  local copies, waits for them, and re-layouts  18.8 us (5%)
  between operations  18.3 us (5%)
  starting transfers between devices  9.34 us (3%)
    unnamed x2, waiting for transfers between devices  74 us
    all_gather x1, blocking collectives, body(): lax.all_gather(cn, ('row', 'col'), axis=0, tiled=True)  57 us
    dot_general x6, matrix products, attend(): jnp.dot(queries[:, low:low + HEAD], keys[:, low:low + HEAD].T, preferred_...  52.5 us
    dot_general x6, matrix products, attend(): jnp.dot(weights, values[:, low:low + HEAD], preferred_element_type=jnp.fl...  41.3 us
    reduce_sum x4, other arithmetic, attend(): jnp.sum(expo, axis=-1, keepdims=True)  23.8 us
    ppermute x2, waiting for transfers between devices, with_halo(): before = lax.ppermute(last, axis, up)  15.6 us
    concatenate x2, other arithmetic, with_halo(): x = jnp.concatenate([before, x, after], axis=dim)  10.2 us
    ppermute x2, waiting for transfers between devices, with_halo(): after = lax.ppermute(initial, axis, down)  9.45 us
  transfers between devices with their start and end apart: 5, of which 5 were waited for; matrix products, arithmetic and copies ran while one was open for 2% of the time, Pallas kernels for 0%

commit v1 on v0

--- a/solution.py
+++ b/solution.py
@@ -2,10 +2,19 @@
 import jax.numpy as jnp
 from jax import lax
 from jax.sharding import PartitionSpec as P
+from jax.lax import all_to_all, axis_size
 
 HEAD = 64
 TILE = 32
 POOL = 8
+
+
+def return_all_kinds_here(message):
+    long_array = all_to_all(
+        jnp.stack([message for _ in range(axis_size(("row", "col")))]), ("row", "col"), 0, 0
+    )
+    outer = jnp.concatenate(long_array, axis=0)
+    return outer
 
 
 def with_halo(x, sides, width):
@@ -140,10 +149,7 @@
     local_width = coarse_qkv.shape[2]
     local_heads = local_width // HEAD
     proj = jnp.einsum(
-        "nd,kde->kne",
-        lax.all_gather(cn, ("row", "col"), axis=0, tiled=True),
-        coarse_qkv,
-        preferred_element_type=jnp.float32,
+        "nd,kde->kne", return_all_kinds_here(cn), coarse_qkv, preferred_element_type=jnp.float32
     )
     q_part = cosine(proj[0], local_heads)
     k_part = cosine(proj[1], local_heads)

time: 354 us -> 315 us (0.89)
  blocking collectives: 57 us -> 0 us
  starting transfers between devices: 9.34 us -> 22.8 us
  waiting for transfers between devices: 99.1 us -> 105 us
    all_gather x1 -> x0, blocking collectives: 57 us -> none  [body(): lax.all_gather(cn, ('row', 'col'), axis=0, tiled=True)]
    all_to_all x0 -> x1, starting transfers between devices: none -> 13.4 us  [return_all_kinds_here(): all_to_all(jnp.stack([message for _ in range(axis_size(('row', 'col')))])...]
    all_to_all x0 -> x1, waiting for transfers between devices: none -> 8.31 us  [return_all_kinds_here(): all_to_all(jnp.stack([message for _ in range(axis_size(('row', 'col')))])...]
    unnamed x2, waiting for transfers between devices: 74 us -> 67.8 us
    ppermute x2, waiting for transfers between devices: 15.6 us -> 19.8 us  [with_halo(): before = lax.ppermute(last, axis, up)]
  transfers between devices with their start and end apart: 5 -> 6, of which waited for: 5 -> 6; matrix products, arithmetic and copies ran while one was open for 2% -> 2% of each run, Pallas kernels for 0% -> 0%
where the time goes in v1:
time: 315 us; the launch traced here: 314 us
  waiting for transfers between devices  105 us (33%)
  matrix products  104 us (33%)
  other arithmetic  44.3 us (14%)
  starting transfers between devices  22.8 us (7%)
  local copies, waits for them, and re-layouts  18.6 us (6%)
  between operations  18.4 us (6%)
    unnamed x2, waiting for transfers between devices  67.8 us
    dot_general x6, matrix products, attend(): jnp.dot(queries[:, low:low + HEAD], keys[:, low:low + HEAD].T, preferred_...  52.5 us
    dot_general x6, matrix products, attend(): jnp.dot(weights, values[:, low:low + HEAD], preferred_element_type=jnp.fl...  41.3 us
    reduce_sum x4, other arithmetic, attend(): jnp.sum(expo, axis=-1, keepdims=True)  23.8 us
    ppermute x2, waiting for transfers between devices, with_halo(): before = lax.ppermute(last, axis, up)  19.8 us
    all_to_all x1, starting transfers between devices, return_all_kinds_here(): all_to_all(jnp.stack([message for _ in range(axis_size(('row', 'col')))])...  13.4 us
    concatenate x2, other arithmetic, with_halo(): x = jnp.concatenate([before, x, after], axis=dim)  10.2 us
    ppermute x2, waiting for transfers between devices, with_halo(): after = lax.ppermute(initial, axis, down)  9.44 us
  transfers between devices with their start and end apart: 6, of which 6 were waited for; matrix products, arithmetic and copies ran while one was open for 2% of the time, Pallas kernels for 0%

profile of v1, /device:TPU:2, one launch (start us, length us, event | category | flops | bytes accessed | tf_op | source)
XLA Modules:
  0.0 313.7 jit_solution(9509830773761698276)
XLA Ops:
  14.3 1.7 mul.196
  15.9 1.9 reduce_sum.123
  20.3 2.2 mul.197
  25.1 1.8 collective-permute-start
  28.3 3.6 %collective-permute-done.1 = bf16[2,32,32,128]{3,2,1,0:T(8,128)(2,1)S(1)} collective-permute-done((bf16[2,32,32,128]{3,2,1,0:T(8,128)(2,1)S(1)}, bf16[2,32,32,128]{3,2,1,0:T(8,128)(2,1)S(1)}, u32[]{:S(2)}, u32[]{:S(2)}) %collective-permute-start.1) | collective-permute-done | bytes 524320 | tf_op jit(solution)/shard_map/ppermute | solution.py:28
  33.3 5.0 %collective-permute-start.2 = (bf16[2,96,32,128]{3,2,1,0:T(8,128)(2,1)}, bf16[2,96,32,128]{3,2,1,0:T(8,128)(2,1)}, u32[]{:S(2)}, u32[]{:S(2)}) collective-permute-start(bf16[2,96,32,128]{3,2,1,0:T(8,128)(2,1)} %pad_maximum_fusion.2), channel_id=1, source_target_pairs={{0,1},{1,2},{2,3},{3,4},{4,5},{5,6},{6,7},{8,9},{9,10},{10,11},{11... | collective-permute-start | bytes 4718600 | tf_op jit(solution)/shard_map/ppermute | solution.py:27
  45.9 19.6 %collective-permute-done.2 = bf16[2,96,32,128]{3,2,1,0:T(8,128)(2,1)} collective-permute-done((bf16[2,96,32,128]{3,2,1,0:T(8,128)(2,1)}, bf16[2,96,32,128]{3,2,1,0:T(8,128)(2,1)}, u32[]{:S(2)}, u32[]{:S(2)}) %collective-permute-start.2) | collective-permute-done | bytes 1572896 | tf_op jit(solution)/shard_map/ppermute | solution.py:27
  65.5 5.8 %collective-permute-done.3 = bf16[2,96,32,128]{3,2,1,0:T(8,128)(2,1)} collective-permute-done((bf16[2,96,32,128]{3,2,1,0:T(8,128)(2,1)}, bf16[2,96,32,128]{3,2,1,0:T(8,128)(2,1)}, u32[]{:S(2)}, u32[]{:S(2)}) %collective-permute-start.3) | collective-permute-done | bytes 1572896 | tf_op jit(solution)/shard_map/ppermute | solution.py:28
  71.3 8.8 %pad_maximum_fusion.1 = bf16[2,96,96,128]{3,2,1,0:T(8,128)(2,1)S(1)} fusion(bf16[2,96,32,128]{3,2,1,0:T(8,128)(2,1)} %collective-permute-done.3, bf16[2,32,32,128]{3,2,1,0:T(8,128)(2,1)S(1)} %collective-permute-done.1, bf16[1,32,32,128]{3,2,1,0:T(8,128)(2,1)S(1)} %fusion.38, bf16[1,32,32,128]{3,2,1,0:T(8,128)(2,1)S(1)} %fusion.37, ...), kind=kLoop, calls=%fused_computation.33 | loop fusion | flops 28311552 | bytes 9437184 | tf_op jit(solution)/shard_map/concatenate | solution.py:29
  80.2 2.2 fusion.71
  82.4 118.7 %while.13 = (s32[]{:T(128)}, bf16[2,512,128]{2,1,0:T(8,128)(2,1)}, bf16[2,512,128]{2,1,0:T(8,128)(2,1)S(1)}, bf16[9216,128]{1,0:T(8,128)(2,1)S(1)}, f32[]{:T(128...) while((s32[]{:T(128)}, bf16[2,512,128]{2,1,0:T(8,128)(2,1)}, ...), condition=%wide.region_8.9_spmd.clone, body=%wide.region_3.8_spmd.clone.sunk | while | flops 2548374528 | bytes 133657432 | solution.py:73
  82.8 7.8 %fusion.103 = (f32[512]{0:T(512)S(1)}, f32[512,9216]{1,0:T(8,128)}) fusion(f32[]{:T(128)} %get-tuple-element.291, pred[9216]{0:T(1024)(128)(4,1)S(1)} %broadcast_in_dim.143, bf16[9216,128]{1,0:T(8,128)(2,1)S(1)} %get-tuple-element.290, bf16[512,128]{1,0:T(8,128)(2,1)S(1)} %dynamic-slice_bitcast_fusion.2), kind=kOutput, calls=%fused_computation.7.clone.1 | convolution fusion | flops 618135040 | bytes 21376004 | tf_op jit(solution)/shard_map/while/body/eval_jaxpr/dot_general | solution.py:46
  90.7 18.1 %fusion.104 = (f32[512]{0:T(512)S(1)}, f32[512]{0:T(512)S(1)}, f32[512,9216]{1,0:T(8,128)}) fusion(f32[512,9216]{1,0:T(8,128)} %get-tuple-element.262, f32[512]{0:T(512)S(1)} %get-tuple-element.263, f32[]{:T(128)} %get-tuple-element.291, pred[9216]{0:T(1024)(128)(4,1)S(1)} %broadcast_in_dim.143, f32[]{:T(128)} %get-tuple-element.293, ...), kind=kOutput, calls=%fused_computation.9.clone.1 | convolution fusion | flops 641727488 | bytes 40254472 | tf_op jit(solution)/shard_map/while/body/eval_jaxpr/dot_general | solution.py:46
  108.8 9.4 %fusion.107 = bf16[1,512,64]{1,2,0:T(8,128)(2,1)S(1)} fusion(bf16[9216,128]{1,0:T(8,128)(2,1)S(1)} %copy-done.4, f32[512,9216]{1,0:T(8,128)} %get-tuple-element.262, f32[512]{0:T(512)S(1)} %get-tuple-element.266, f32[512]{0:T(512)S(1)} %get-tuple-element.263, f32[]{:T(128)} %get-tuple-element.291, pred[9216]{0:T(1024)(128)(4,1)S(1)} %broadcast_in_dim.143), kind=kOutput, calls=%fused_computation.21.clone.1 | convolution fusion | flops 632324096 | bytes 21312516 | tf_op jit(solution)/shard_map/while/body/eval_jaxpr/dot_general | solution.py:60
  118.2 11.7 %fusion.105 = f32[512]{0:T(512)S(1)} fusion(f32[512,9216]{1,0:T(8,128)} %get-tuple-element.264, f32[512]{0:T(512)S(1)} %get-tuple-element.265, f32[]{:T(128)} %get-tuple-element.293, pred[9216]{0:T(1024)(128)(4,1)S(1)} %broadcast_in_dim.143), kind=kLoop, calls=%fused_computation.10.clone.1 | loop fusion | flops 23592448 | bytes 18887684 | tf_op jit(solution)/shard_map/while/body/eval_jaxpr/reduce_sum | solution.py:58
  129.9 11.1 %fusion.106 = bf16[1,512,64]{1,2,0:T(8,128)(2,1)S(1)} fusion(bf16[9216,128]{1,0:T(8,128)(2,1)} %get-tuple-element.292, f32[512,9216]{1,0:T(8,128)} %get-tuple-element.264, f32[512]{0:T(512)S(1)} %fusion.105, f32[512]{0:T(512)S(1)} %get-tuple-element.265, f32[]{:T(128)} %get-tuple-element.293, pred[9216]{0:T(1024)(128)(4,1)S(1)} %broadcast_in_dim.143), kind=kOutput, calls=%fused_computation.22.clone.1 | convolution fusion | flops 632324096 | bytes 21312516 | tf_op jit(solution)/shard_map/while/body/eval_jaxpr/dot_general | solution.py:60
  142.0 7.8 %fusion.103 = (f32[512]{0:T(512)S(1)}, f32[512,9216]{1,0:T(8,128)}) fusion(f32[]{:T(128)} %get-tuple-element.291, pred[9216]{0:T(1024)(128)(4,1)S(1)} %broadcast_in_dim.143, bf16[9216,128]{1,0:T(8,128)(2,1)S(1)} %get-tuple-element.290, bf16[512,128]{1,0:T(8,128)(2,1)S(1)} %dynamic-slice_bitcast_fusion.2), kind=kOutput, calls=%fused_computation.7.clone.1 | convolution fusion | flops 618135040 | bytes 21376004 | tf_op jit(solution)/shard_map/while/body/eval_jaxpr/dot_general | solution.py:46
  149.9 18.1 %fusion.104 = (f32[512]{0:T(512)S(1)}, f32[512]{0:T(512)S(1)}, f32[512,9216]{1,0:T(8,128)}) fusion(f32[512,9216]{1,0:T(8,128)} %get-tuple-element.262, f32[512]{0:T(512)S(1)} %get-tuple-element.263, f32[]{:T(128)} %get-tuple-element.291, pred[9216]{0:T(1024)(128)(4,1)S(1)} %broadcast_in_dim.143, f32[]{:T(128)} %get-tuple-element.293, ...), kind=kOutput, calls=%fused_computation.9.clone.1 | convolution fusion | flops 641727488 | bytes 40254472 | tf_op jit(solution)/shard_map/while/body/eval_jaxpr/dot_general | solution.py:46
  168.0 9.4 %fusion.107 = bf16[1,512,64]{1,2,0:T(8,128)(2,1)S(1)} fusion(bf16[9216,128]{1,0:T(8,128)(2,1)S(1)} %copy-done.4, f32[512,9216]{1,0:T(8,128)} %get-tuple-element.262, f32[512]{0:T(512)S(1)} %get-tuple-element.266, f32[512]{0:T(512)S(1)} %get-tuple-element.263, f32[]{:T(128)} %get-tuple-element.291, pred[9216]{0:T(1024)(128)(4,1)S(1)} %broadcast_in_dim.143), kind=kOutput, calls=%fused_computation.21.clone.1 | convolution fusion | flops 632324096 | bytes 21312516 | tf_op jit(solution)/shard_map/while/body/eval_jaxpr/dot_general | solution.py:60
  177.4 11.7 %fusion.105 = f32[512]{0:T(512)S(1)} fusion(f32[512,9216]{1,0:T(8,128)} %get-tuple-element.264, f32[512]{0:T(512)S(1)} %get-tuple-element.265, f32[]{:T(128)} %get-tuple-element.293, pred[9216]{0:T(1024)(128)(4,1)S(1)} %broadcast_in_dim.143), kind=kLoop, calls=%fused_computation.10.clone.1 | loop fusion | flops 23592448 | bytes 18887684 | tf_op jit(solution)/shard_map/while/body/eval_jaxpr/reduce_sum | solution.py:58
  189.2 11.1 %fusion.106 = bf16[1,512,64]{1,2,0:T(8,128)(2,1)S(1)} fusion(bf16[9216,128]{1,0:T(8,128)(2,1)} %get-tuple-element.292, f32[512,9216]{1,0:T(8,128)} %get-tuple-element.264, f32[512]{0:T(512)S(1)} %fusion.105, f32[512]{0:T(512)S(1)} %get-tuple-element.265, f32[]{:T(128)} %get-tuple-element.293, pred[9216]{0:T(1024)(128)(4,1)S(1)} %broadcast_in_dim.143), kind=kOutput, calls=%fused_computation.22.clone.1 | convolution fusion | flops 632324096 | bytes 21312516 | tf_op jit(solution)/shard_map/while/body/eval_jaxpr/dot_general | solution.py:60
  207.5 13.4 %all-to-all-start = ((bf16[32,4,1024]{2,1,0:T(4,128)(2,1)}), bf16[32,4,1024]{2,1,0:T(4,128)(2,1)S(1)}, u32[]{:S(2)}, u32[]{:S(2)}) async-start(bf16[32,4,1024]{2,1,0:T(4,128)(2,1)} %stack.11), calls=%async_computation | async-start | bytes 524288 | tf_op jit(solution)/shard_map/all_to_all | solution.py:13
  224.3 8.3 %all-to-all-done = bf16[32,4,1024]{2,1,0:T(4,128)(2,1)S(1)} async-done(((bf16[32,4,1024]{2,1,0:T(4,128)(2,1)}), bf16[32,4,1024]{2,1,0:T(4,128)(2,1)S(1)}, u32[]{:S(2)}, u32[]{:S(2)}) %all-to-all-start) | async-done | bytes 262176 | tf_op jit(solution)/shard_map/all_to_all | solution.py:13
  236.7 67.8 %all-reduce.3.cloned.1.call-done = bf16[32,1024]{1,0:T(8,128)(2,1)} async-done(((bf16[32,1024]{1,0:T(8,128)(2,1)}), bf16[32,1024]{1,0:T(8,128)(2,1)}) %all-reduce.3.cloned.1.call-update) | async-done | bytes 65552
  (112 shorter events, 36.5 us)
Async XLA Ops:
  7.2 37.5 %copy-start = (f32[256,1024]{1,0:T(8,128)S(1)}, f32[256,1024]{1,0:T(8,128)}, u32[]{:S(2)}) copy-start(f32[256,1024]{1,0:T(8,128)} %param.27) | copy-start | bytes 3145732
  12.2 2.1 copy-start.3
  12.2 30.6 %copy-start.10 = (f32[2]{0:T(128)S(1)}, f32[2]{0:T(128)}, u32[]{:S(2)}) copy-start(f32[2]{0:T(128)} %param.22) | copy-start | bytes 28
  25.1 3.3 %collective-permute-start = (bf16[2,32,32,128]{3,2,1,0:T(8,128)(2,1)S(1)}, bf16[2,32,32,128]{3,2,1,0:T(8,128)(2,1)S(1)}, u32[]{:S(2)}, u32[]{:S(2)}) collective-permute-start(bf16[2,32,32,128]{3,2,1,0:T(8,128)(2,1)S(1)} %pad_maximum_fusion.3), channel_id=1, source_target_pairs={{0,8},{8,16},{16,24},{1,9},{9,17},{17,25},{2,10},{10,18},{18,26},{... | collective-permute-start | bytes 1572872 | tf_op jit(solution)/shard_map/ppermute | solution.py:27
  26.8 5.1 %collective-permute-start.1 = (bf16[2,32,32,128]{3,2,1,0:T(8,128)(2,1)S(1)}, bf16[2,32,32,128]{3,2,1,0:T(8,128)(2,1)S(1)}, u32[]{:S(2)}, u32[]{:S(2)}) collective-permute-start(bf16[2,32,32,128]{3,2,1,0:T(8,128)(2,1)S(1)} %pad_maximum_fusion.3), channel_id=1, source_target_pairs={{8,0},{16,8},{24,16},{9,1},{17,9},{25,17},{10,2},{18,10},{26,18},{... | collective-permute-start | bytes 1572872 | tf_op jit(solution)/shard_map/ppermute | solution.py:28
  33.3 32.2 %collective-permute-start.2 = (bf16[2,96,32,128]{3,2,1,0:T(8,128)(2,1)}, bf16[2,96,32,128]{3,2,1,0:T(8,128)(2,1)}, u32[]{:S(2)}, u32[]{:S(2)}) collective-permute-start(bf16[2,96,32,128]{3,2,1,0:T(8,128)(2,1)} %pad_maximum_fusion.2), channel_id=1, source_target_pairs={{0,1},{1,2},{2,3},{3,4},{4,5},{5,6},{6,7},{8,9},{9,10},{10,11},{11... | collective-permute-start | bytes 4718600 | tf_op jit(solution)/shard_map/ppermute | solution.py:27
  38.3 33.1 %collective-permute-start.3 = (bf16[2,96,32,128]{3,2,1,0:T(8,128)(2,1)}, bf16[2,96,32,128]{3,2,1,0:T(8,128)(2,1)}, u32[]{:S(2)}, u32[]{:S(2)}) collective-permute-start(bf16[2,96,32,128]{3,2,1,0:T(8,128)(2,1)} %pad_maximum_fusion.2), channel_id=1, source_target_pairs={{1,0},{2,1},{3,2},{4,3},{5,4},{6,5},{7,6},{9,8},{10,9},{11,10},{12... | collective-permute-start | bytes 4718600 | tf_op jit(solution)/shard_map/ppermute | solution.py:28
  45.9 36.5 %copy-start.2 = (bf16[2,512,128]{2,1,0:T(8,128)(2,1)S(1)}, bf16[2,512,128]{2,1,0:T(8,128)(2,1)}, u32[]{:S(2)}) copy-start(bf16[2,512,128]{2,1,0:T(8,128)(2,1)} %copy.39) | copy-start | bytes 786436
  82.4 118.7 %copy-start.7 = (bf16[128,128]{1,0:T(8,128)(2,1)S(1)}, bf16[128,128]{1,0:T(8,128)(2,1)}, u32[]{:S(2)}) copy-start(bf16[128,128]{1,0:T(8,128)(2,1)} %param.23) | copy-start | bytes 98308
  82.4 120.1 %copy-start.12 = (f32[128]{0:T(128)S(1)}, f32[128]{0:T(128)}, u32[]{:S(2)}) copy-start(f32[128]{0:T(128)} %param.24) | copy-start | bytes 1540
  82.4 124.2 %copy-start.8 = (f32[1024]{0:T(1024)S(1)}, f32[1024]{0:T(1024)}, u32[]{:S(2)}) copy-start(f32[1024]{0:T(1024)} %broadcast_add_fusion) | copy-start | bytes 12292
  82.4 140.0 %copy-start.11 = (f32[2]{0:T(128)S(1)}, f32[2]{0:T(128)}, u32[]{:S(2)}) copy-start(f32[2]{0:T(128)} %param.29) | copy-start | bytes 28
  90.6 18.1 %copy-start.4 = (bf16[9216,128]{1,0:T(8,128)(2,1)S(1)}, bf16[9216,128]{1,0:T(8,128)(2,1)}, u32[]{:S(2)}) copy-start(bf16[9216,128]{1,0:T(8,128)(2,1)} %get-tuple-element.292) | copy-start | bytes 7077892 | tf_op jit(solution)/shard_map/while
  149.9 18.2 %copy-start.4 = (bf16[9216,128]{1,0:T(8,128)(2,1)S(1)}, bf16[9216,128]{1,0:T(8,128)(2,1)}, u32[]{:S(2)}) copy-start(bf16[9216,128]{1,0:T(8,128)(2,1)} %get-tuple-element.292) | copy-start | bytes 7077892 | tf_op jit(solution)/shard_map/while
  201.1 33.6 %copy-start.6 = (bf16[128,1024]{1,0:T(8,128)(2,1)S(1)}, bf16[128,1024]{1,0:T(8,128)(2,1)}, u32[]{:S(2)}) copy-start(bf16[128,1024]{1,0:T(8,128)(2,1)} %param.30) | copy-start | bytes 786436
  201.1 34.4 %copy-start.13 = (u32[256]{0:T(256)S(1)}, u32[256]{0:T(256)}, u32[]{:S(2)}) copy-start(u32[256]{0:T(256)} %constant.97) | copy-start | bytes 3076
  201.1 104.3 %copy-start.9 = (f32[1024]{0:T(1024)S(1)}, f32[1024]{0:T(1024)}, u32[]{:S(2)}) copy-start(f32[1024]{0:T(1024)} %param.31) | copy-start | bytes 12292
  201.1 105.7 %copy-start.1 = (f32[256,1024]{1,0:T(8,128)S(1)}, f32[256,1024]{1,0:T(8,128)}, u32[]{:S(2)}) copy-start(f32[256,1024]{1,0:T(8,128)} %param.27) | copy-start | bytes 3145732
  203.7 103.1 %copy-start.5 = (bf16[32,32,128]{2,1,0:T(8,128)(2,1)}, bf16[32,32,128]{2,1,0:T(8,128)(2,1)S(1)}, u32[]{:S(2)}) copy-start(bf16[32,32,128]{2,1,0:T(8,128)(2,1)S(1)} %fusion.36) | copy-start | bytes 786436
  207.5 25.1 %all-to-all-start = ((bf16[32,4,1024]{2,1,0:T(4,128)(2,1)}), bf16[32,4,1024]{2,1,0:T(4,128)(2,1)S(1)}, u32[]{:S(2)}, u32[]{:S(2)}) async-start(bf16[32,4,1024]{2,1,0:T(4,128)(2,1)} %stack.11), calls=%async_computation | async-start | bytes 524288 | tf_op jit(solution)/shard_map/all_to_all | solution.py:13
  220.9 83.7 %all-reduce.3.cloned.1.call-start = ((), (), s32[]{:S(2)}) async-start(), calls=%async_computation.1 | async-start | bytes 131072
Sparse Core Ops, SparseCore 0:
  235.6 68.8 all-reduce.2
